TPU v7x, 32 devices: a whole 2x2x4 slice. The times are simulated.
32 devices in a mesh: expert: 8 (over y, x, core), tensor: 4 (over z).
Axes of the slice: x: 2, y: 2, z: 4, core: 2. Of those that a mesh axis runs over, the one named last changes fastest.
Arguments:
- tokens: bfloat16 [2560, 4096], P('expert', 'tensor'), may hold values from -6 to 6
- grad_out: bfloat16 [2560, 4096], P('expert', 'tensor'), may hold values from -6 to 6
- routes: int32 [2560, 4], P('expert'), may hold values from 0 to 7, all different within a row; in each aligned block of 320 rows (0 to 319, 320 to 639, ...) at most 200 rows name the same one
- route_weights: float32 [2560, 4], P('expert'), may hold values from 0.05 to 0.5
- swap_flags: int32 [4], replicated, may hold values from 0 to 1023
- weights: bfloat16 [8, 3, 1536, 4096], P('expert', None, None, 'tensor'), may hold values from -0.09375 to 0.09375
- first_moment: bfloat16 [8, 3, 1536, 4096], P('expert', None, None, 'tensor'), may hold values from -8 to 8
- second_moment: bfloat16 [8, 3, 1536, 4096], P('expert', None, None, 'tensor'), may hold values from 1 to 30
Outputs:
- combined: bfloat16 [2560, 4096], P('expert', 'tensor')
- update: bfloat16 [8, 3, 1536, 4096], P('expert', None, None, 'tensor')
Inputs may be any that keep to these rules, and one draw needn't show every extreme that they name: `routes`: in each aligned block of 320 rows no expert is named by more than 200 rows, a bound that some block reaches; a row names 4 different experts.
All inputs are finite; a program needn't handle non-finite values.
Results may differ from a plain program's by a relative error of at most 0.023.
Values may be sent and summed in bfloat16 or wider, within the bound.
A program may use at most 192 MiB of HBM per device.

v0:
```python
import jax
import jax.numpy as jnp
from jax import lax
from jax.sharding import PartitionSpec as P

correction_one = 1.0 - 0.9**20
correction_two = 1.0 - 0.95**20


def from_partner(value, axis, distance):
    return lax.ppermute(value, axis, [(i, i ^ 1 << distance) for i in range(lax.axis_size(axis))])


def contract_last(left_rows, right_rows):
    return lax.dot_general(
        left_rows, right_rows, (((1,), (1,)), ((), ())), preferred_element_type=jnp.float32
    )


def contract_first(left_rows, right_rows):
    return lax.dot_general(
        left_rows, right_rows, (((0,), (0,)), ((), ())), preferred_element_type=jnp.float32
    )


def body(tokens, grad_out, routes, route_weights, swap_flags, weights, first_moment, second_moment):
    expert_count = lax.axis_size("expert")
    tok_count = routes.shape[0]
    route_count = routes.shape[1]
    feat_width = tokens.shape[1]
    slot_cap = tok_count * route_count * 5 // (4 * expert_count)
    slot_total = tok_count * route_count
    positions = jnp.arange(expert_count, dtype=jnp.int32)
    paired = jnp.repeat(jnp.bitwise_and(swap_flags, 1), 2)
    own_flag = jnp.sum(jnp.where(positions == lax.axis_index("expert"), paired, 0))
    moved = from_partner((weights, first_moment, second_moment), "expert", 0)
    traded = own_flag == 1
    weights = jnp.where(traded, moved[0], weights)
    first_moment = jnp.where(traded, moved[1], first_moment)
    second_moment = jnp.where(traded, moved[2], second_moment)
    destination = jnp.where(paired == 1, jnp.bitwise_xor(positions, 1), positions)
    flat_ids = routes.reshape(-1)
    id_onehot = (flat_ids[:, None] == positions[None, :]).astype(jnp.int32)
    dest_ids = jnp.sum(id_onehot * destination[None, :], axis=1)
    dest_onehot = (dest_ids[:, None] == positions[None, :]).astype(jnp.int32)
    slot_rank = jnp.sum((jnp.cumsum(dest_onehot, axis=0) - dest_onehot) * dest_onehot, axis=1)
    slot_index = dest_ids * slot_cap + slot_rank
    table_rows = (
        jnp.full((expert_count * slot_cap,), slot_total, jnp.int32)
        .at[slot_index]
        .set(jnp.arange(slot_total, dtype=jnp.int32))
    )
    token_pad = jnp.concatenate([tokens, jnp.zeros((1, feat_width), tokens.dtype)], axis=0)
    scaled_grad = (route_weights[:, :, None] * grad_out[:, None, :].astype(jnp.float32)).astype(
        jnp.bfloat16
    )
    grad_pad = jnp.concatenate(
        [scaled_grad.reshape(slot_total, feat_width), jnp.zeros((1, feat_width), jnp.bfloat16)],
        axis=0,
    )
    send_tokens = token_pad[table_rows // route_count].reshape(expert_count, slot_cap, feat_width)
    send_grads = grad_pad[table_rows].reshape(expert_count, slot_cap, feat_width)
    got_tokens, got_grads = (
        lax.all_to_all(send_tokens, "expert", split_axis=0, concat_axis=0, tiled=True),
        lax.all_to_all(send_grads, "expert", split_axis=0, concat_axis=0, tiled=True),
    )
    slot_rows = expert_count * slot_cap
    token_slots = got_tokens.reshape(slot_rows, feat_width)
    grad_slots = got_grads.reshape(slot_rows, feat_width)
    own_weights = weights[0]
    hidden_width = own_weights.shape[1]
    preact = lax.psum(
        contract_last(token_slots, own_weights[0:2].reshape(2 * hidden_width, feat_width)).astype(
            jnp.bfloat16
        ),
        "tensor",
    ).astype(jnp.float32)
    gate_pre = preact[:, :hidden_width]
    up_pre = preact[:, hidden_width:]
    sig_gate = jax.nn.sigmoid(gate_pre)
    hidden = (gate_pre * sig_gate * up_pre).astype(jnp.bfloat16)
    output_slots = jnp.dot(hidden, own_weights[2], preferred_element_type=jnp.float32).astype(
        jnp.bfloat16
    )
    returned = lax.all_to_all(
        output_slots.reshape(expert_count, slot_cap, feat_width),
        "expert",
        split_axis=0,
        concat_axis=0,
        tiled=True,
    )
    hidden_grad = lax.psum(
        contract_last(grad_slots, own_weights[2]).astype(jnp.bfloat16), "tensor"
    ).astype(jnp.float32)
    gate_grad = (hidden_grad * up_pre * sig_gate * (1.0 + gate_pre * (1.0 - sig_gate))).astype(
        jnp.bfloat16
    )
    up_grad = (hidden_grad * gate_pre * sig_gate).astype(jnp.bfloat16)
    weight_grad = jnp.stack(
        [
            contract_first(gate_grad, token_slots),
            contract_first(up_grad, token_slots),
            contract_first(hidden, grad_slots),
        ]
    )
    moment_new = 0.9 * first_moment[0].astype(jnp.float32) + 0.1 * weight_grad
    square_new = 0.95 * second_moment[0].astype(jnp.float32) + 0.05 * weight_grad * weight_grad
    step_dir = moment_new / correction_one / (jnp.sqrt(square_new / correction_two) + 1e-08)
    update = step_dir.astype(jnp.bfloat16)[None]
    back_slots = returned.reshape(slot_rows, feat_width)
    gathered_out = (
        back_slots[slot_index].reshape(tok_count, route_count, feat_width).astype(jnp.float32)
    )
    combined = jnp.sum(route_weights[:, :, None] * gathered_out, axis=1).astype(jnp.bfloat16)
    return (combined, update)


def solution(mesh):
    placed = (
        P("expert", "tensor"),
        P("expert", "tensor"),
        P("expert", None),
        P("expert", None),
        P(),
        P("expert", None, None, "tensor"),
        P("expert", None, None, "tensor"),
        P("expert", None, None, "tensor"),
    )
    return jax.shard_map(
        body,
        mesh=mesh,
        in_specs=placed,
        out_specs=(P("expert", "tensor"), P("expert", None, None, "tensor")),
        check_vma=False,
    )
```

profile of v0, /device:TPU:0, one launch (start us, length us, event | category | flops | bytes accessed | tf_op | source)
XLA Modules:
  0.0 758.2 jit_solution(17305862190993749333)
XLA Ops:
  7.2 0.0 copy-start.7
  7.2 0.6 collective-permute-start
  7.7 0.7 broadcast_compare_fusion
  8.4 0.1 broadcast_in_dim.15
  8.5 0.1 eq.64
  8.6 0.8 copy.15
  9.4 0.1 eq.59
  9.5 0.1 select_reduce_fusion
  9.6 2.3 reduce-window.6
  11.9 0.3 slice_reduce_fusion
  12.2 0.2 reduce-window.9
  12.4 4.9 mul.138
  17.2 7.3 mul.139
  24.5 0.0 copy-done.7
  24.5 0.1 copy.14
  24.7 0.0 copy-start.4
  24.7 0.1 mul.136
  24.8 0.5 copy-done.4
  25.3 2.8 multiply_convert_fusion.1
  28.2 0.2 concatenate.26
  28.4 0.1 add_bitcast_fusion
  28.6 5.2 scatter_custom_fusion
  33.9 0.0 copy-start.6
  33.9 6.4 gather_fusion.2
  40.3 4.8 all-to-all-start.2
  45.1 0.0 copy-done.6
  45.2 0.0 copy-start.8
  45.2 6.5 gather_fusion
  51.7 33.2 %all-to-all-done.2 = bf16[8,200,1024]{2,1,0:T(8,128)(2,1)} async-done(((bf16[8,200,1024]{2,1,0:T(8,128)(2,1)}), bf16[8,200,1024]{2,1,0:T(8,128)(2,1)}, u32[]{:S(2)}, u32[]{:S(2)}) %all-to-all-start.2) | async-done | bytes 3276832 | tf_op jit(solution)/shard_map/all_to_all | solution.py:65
  85.0 3.7 all-to-all-start
  88.6 0.2 all-reduce.5.cloned.1.call-start
  88.8 0.0 copy-done.8
  88.9 0.6 fusion.30
  90.2 0.0 collective-permute-done
  90.2 5.4 broadcast_select_fusion
  95.6 0.0 copy-start
  95.6 3.8 slice.34
  99.4 1.8 copy-done
  101.2 9.0 %convolution_convert_fusion.1 = bf16[1600,1536]{1,0:T(8,128)(2,1)} fusion(bf16[1600,1024]{1,0:T(8,128)(2,1)} %bitcast.9, bf16[1,3,1536,1024]{3,2,1,0:T(8,128)(2,1)S(1)} %broadcast_select_fusion), kind=kOutput, calls=%fused_computation.23 | convolution fusion | flops 5035622400 | bytes 11337728 | tf_op jit(solution)/shard_map/dot_general | solution.py:15
  110.2 17.6 %all-to-all-done = bf16[8,200,1024]{2,1,0:T(8,128)(2,1)S(1)} async-done(((bf16[8,200,1024]{2,1,0:T(8,128)(2,1)}), bf16[8,200,1024]{2,1,0:T(8,128)(2,1)S(1)}, u32[]{:S(2)}, u32[]{:S(2)}) %all-to-all-start) | async-done | bytes 3276832 | tf_op jit(solution)/shard_map/all_to_all | solution.py:64
  127.8 16.5 %convolution_convert_fusion = bf16[1600,3072]{1,0:T(8,128)(2,1)} fusion(bf16[1600,1024]{1,0:T(8,128)(2,1)S(1)} %bitcast.51, bf16[3072,1024]{1,0:T(8,128)(2,1)} %bitcast.50), kind=kOutput, calls=%fused_computation.14 | convolution fusion | flops 10071244800 | bytes 19398656 | tf_op jit(solution)/shard_map/dot_general | solution.py:15
  144.3 0.0 copy-done.2
  144.3 0.0 all-reduce.5.cloned.1.call-update
  144.3 0.1 collective-permute-start.2
  144.4 0.5 collective-permute-start.1
  144.9 494.9 %all-reduce.5.cloned.1.call-done = (bf16[1600,3072]{1,0:T(8,128)(2,1)}, bf16[1600,1536]{1,0:T(8,128)(2,1)}) async-done(((bf16[1600,3072]{1,0:T(8,128)(2,1)}, bf16[1600,1536]{1,0:T(8,128)(2,1)}), (bf16[1600,3072]{1,0:T(8,128)(2,1)}, bf16[1600,1536]{1,0:T(8,128)(2,1)})) %all-reduce.5.cloned.1.call-update) | async-done | bytes 14745616 | tf_op jit(solution)/shard_map/psum | solution.py:72
  639.9 12.8 %convert_element_type.64 = f32[1600,3072]{1,0:T(8,128)} convert(bf16[1600,3072]{1,0:T(8,128)(2,1)} %get-tuple-element.2) | non-fusion elementwise | flops 4915200 | bytes 29491200 | tf_op jit(solution)/shard_map/convert_element_type | solution.py:77
  652.7 8.2 %multiply_convert_fusion = bf16[1600,1536]{1,0:T(8,128)(2,1)S(1)} fusion(f32[1600,3072]{1,0:T(8,128)} %convert_element_type.64), kind=kLoop, calls=%fused_computation.20 | loop fusion | flops 14745600 | bytes 24576000 | tf_op jit(solution)/shard_map/convert_element_type | solution.py:81
  660.8 0.0 copy-start.1
  660.9 10.3 %convolution_convert_fusion.2 = bf16[1600,1024]{1,0:T(8,128)(2,1)} fusion(bf16[1600,1536]{1,0:T(8,128)(2,1)S(1)} %multiply_convert_fusion, bf16[1,3,1536,1024]{3,2,1,0:T(8,128)(2,1)} %copy-done), kind=kOutput, calls=%fused_computation.31 | convolution fusion | flops 5034803200 | bytes 11337728 | tf_op jit(solution)/shard_map/dot_general | solution.py:82
  671.2 3.9 all-to-all-start.1
  675.1 0.0 copy-start.3
  675.1 9.1 %convolution_bitcast_fusion = f32[1,1,1536,1024]{3,2,1,0:T(8,128)S(1)} fusion(bf16[1600,1536]{1,0:T(8,128)(2,1)} %copy-done.1, bf16[1600,1024]{1,0:T(8,128)(2,1)} %bitcast.9), kind=kOutput, calls=%fused_computation.30 | convolution fusion | flops 5033164800 | bytes 14483456 | tf_op jit(solution)/shard_map/dot_general | solution.py:21
  684.2 0.0 slice-start
  684.2 0.0 slice-start.1
  684.2 11.4 %fusion.18 = f32[1,1,1536,1024]{3,2,1,0:T(8,128)} fusion(bf16[1600,1024]{1,0:T(8,128)(2,1)S(1)} %bitcast.53, bf16[1600,1536]{1,0:T(8,128)(2,1)} %get-tuple-element.3, f32[1600,3072]{1,0:T(8,128)} %convert_element_type.64), kind=kOutput, calls=%fused_computation.29 | convolution fusion | flops 5050368000 | bytes 24313856 | tf_op jit(solution)/shard_map/dot_general | solution.py:21
  695.6 16.4 %fusion.15 = f32[1,1,1536,1024]{3,2,1,0:T(8,128)} fusion(bf16[1600,1024]{1,0:T(8,128)(2,1)} %bitcast.52, bf16[1600,1536]{1,0:T(8,128)(2,1)} %get-tuple-element.3, f32[1600,3072]{1,0:T(8,128)} %convert_element_type.64), kind=kOutput, calls=%fused_computation.28 | convolution fusion | flops 5060198400 | bytes 34144256 | tf_op jit(solution)/shard_map/dot_general | solution.py:21
  712.0 0.0 collective-permute-done.2
  712.0 0.0 collective-permute-done.1
  712.1 21.6 %fusion.5 = bf16[1,3,1536,1024]{3,2,1,0:T(8,128)(2,1)} fusion(f32[1,1,1536,1024]{3,2,1,0:T(8,128)S(1)} %convolution_bitcast_fusion, f32[1,1,1536,1024]{3,2,1,0:T(8,128)} %fusion.18, f32[1,1,1536,1024]{3,2,1,0:T(8,128)} %fusion.15, bf16[1,3,1536,1024]{3,2,1,0:T(8,128)(2,1)} %collective-permute-done.2, bf16[1,3,1536,1024]{3,2,1,0:T(8,128)(2,1)S(1)} %bitcast.49, ...), kind=kLoop, calls=%fused_computation.11 | loop fusion | flops 84934656 | bytes 66060288 | tf_op jit(solution)/shard_map/convert_element_type | solution.py:109
  733.7 0.0 all-to-all-done.1
  733.7 5.1 gather_fusion.1
  738.8 5.9 reshape.227
  744.6 6.7 multiply_reduce_fusion
  (21 shorter events, 0.2 us)
Async XLA Ops:
  7.2 17.4 %copy-start.7 = (f32[320,4]{0,1:T(4,128)S(1)}, f32[320,4]{0,1:T(4,128)}, u32[]{:S(2)}) copy-start(f32[320,4]{0,1:T(4,128)} %param.11) | copy-start | bytes 15364
  7.2 83.0 %collective-permute-start = (bf16[1,3,1536,1024]{3,2,1,0:T(8,128)(2,1)}, bf16[1,3,1536,1024]{3,2,1,0:T(8,128)(2,1)}, u32[]{:S(2)}, u32[]{:S(2)}) collective-permute-start(bf16[1,3,1536,1024]{3,2,1,0:T(8,128)(2,1)} %param.13), channel_id=1, source_target_pairs={{0,4},{4,0},{8,12},{12,8},{16,20},{20,16},{24,28},{28,24},{1,5},{5... | collective-permute-start | bytes 28311560 | tf_op jit(solution)/shard_map/ppermute | solution.py:11
  24.7 0.7 copy-start.4
  33.9 11.3 %copy-start.6 = (bf16[320,1024]{1,0:T(8,128)(2,1)S(1)}, bf16[320,1024]{1,0:T(8,128)(2,1)}, u32[]{:S(2)}) copy-start(bf16[320,1024]{1,0:T(8,128)(2,1)} %param.8) | copy-start | bytes 1966084
  40.3 44.6 %all-to-all-start.2 = ((bf16[8,200,1024]{2,1,0:T(8,128)(2,1)}), bf16[8,200,1024]{2,1,0:T(8,128)(2,1)}, u32[]{:S(2)}, u32[]{:S(2)}) async-start(bf16[8,200,1024]{2,1,0:T(8,128)(2,1)} %bitcast.47), calls=%async_computation.2 | async-start | bytes 6553600 | tf_op jit(solution)/shard_map/all_to_all | solution.py:65
  45.2 43.6 %copy-start.8 = (s32[4]{0:T(128)S(1)}, s32[4]{0:T(128)}, u32[]{:S(2)}) copy-start(s32[4]{0:T(128)} %param.12) | copy-start | bytes 52
  85.0 42.9 %all-to-all-start = ((bf16[8,200,1024]{2,1,0:T(8,128)(2,1)}), bf16[8,200,1024]{2,1,0:T(8,128)(2,1)S(1)}, u32[]{:S(2)}, u32[]{:S(2)}) async-start(bf16[8,200,1024]{2,1,0:T(8,128)(2,1)} %bitcast.46), calls=%async_computation | async-start | bytes 6553600 | tf_op jit(solution)/shard_map/all_to_all | solution.py:64
  88.6 551.2 %all-reduce.5.cloned.1.call-start = ((), (), s32[]{:S(2)}) async-start(), calls=%async_computation.3 | async-start | bytes 29491200 | tf_op jit(solution)/shard_map/psum | solution.py:72
  95.6 5.6 copy-start
  127.8 16.5 %copy-start.2 = (bf16[8,200,1024]{2,1,0:T(8,128)(2,1)}, bf16[8,200,1024]{2,1,0:T(8,128)(2,1)S(1)}, u32[]{:S(2)}) copy-start(bf16[8,200,1024]{2,1,0:T(8,128)(2,1)S(1)} %all-to-all-done) | copy-start | bytes 9830404
  144.3 567.7 %collective-permute-start.2 = (bf16[1,3,1536,1024]{3,2,1,0:T(8,128)(2,1)}, bf16[1,3,1536,1024]{3,2,1,0:T(8,128)(2,1)}, u32[]{:S(2)}, u32[]{:S(2)}) collective-permute-start(bf16[1,3,1536,1024]{3,2,1,0:T(8,128)(2,1)} %param.15), channel_id=1, source_target_pairs={{0,4},{4,0},{8,12},{12,8},{16,20},{20,16},{24,28},{28,24},{1,5},{5... | collective-permute-start | bytes 28311560 | tf_op jit(solution)/shard_map/ppermute | solution.py:11
  144.4 567.6 %collective-permute-start.1 = (bf16[1,3,1536,1024]{3,2,1,0:T(8,128)(2,1)}, bf16[1,3,1536,1024]{3,2,1,0:T(8,128)(2,1)}, u32[]{:S(2)}, u32[]{:S(2)}) collective-permute-start(bf16[1,3,1536,1024]{3,2,1,0:T(8,128)(2,1)} %param.14), channel_id=1, source_target_pairs={{0,4},{4,0},{8,12},{12,8},{16,20},{20,16},{24,28},{28,24},{1,5},{5... | collective-permute-start | bytes 28311560 | tf_op jit(solution)/shard_map/ppermute | solution.py:11
  660.8 10.3 %copy-start.1 = (bf16[1600,1536]{1,0:T(8,128)(2,1)}, bf16[1600,1536]{1,0:T(8,128)(2,1)S(1)}, u32[]{:S(2)}) copy-start(bf16[1600,1536]{1,0:T(8,128)(2,1)S(1)} %multiply_convert_fusion) | copy-start | bytes 14745604
  671.2 62.5 %all-to-all-start.1 = ((bf16[8,200,1024]{2,1,0:T(8,128)(2,1)}), bf16[8,200,1024]{2,1,0:T(8,128)(2,1)S(1)}, u32[]{:S(2)}, u32[]{:S(2)}) async-start(bf16[8,200,1024]{2,1,0:T(8,128)(2,1)} %bitcast.54), calls=%async_computation.1 | async-start | bytes 6553600 | tf_op jit(solution)/shard_map/all_to_all | solution.py:85
  675.1 9.1 %copy-start.3 = (bf16[8,200,1024]{2,1,0:T(8,128)(2,1)S(1)}, bf16[8,200,1024]{2,1,0:T(8,128)(2,1)}, u32[]{:S(2)}) copy-start(bf16[8,200,1024]{2,1,0:T(8,128)(2,1)} %copy-done.2) | copy-start | bytes 9830404
  684.2 27.8 %slice-start = ((s8[9437184]{0:T(1024)(128)(4,1)}), s8[4194304]{0:T(1024)(128)(4,1)S(1)}, s32[]{:S(2)}) async-start(s8[9437184]{0:T(1024)(128)(4,1)} %bitcast.48), calls=%async_computation.4 | async-start | bytes 8388608
  684.2 27.8 %slice-start.1 = ((s8[9437184]{0:T(1024)(128)(4,1)}), s8[4194304]{0:T(1024)(128)(4,1)S(1)}, s32[]{:S(2)}) async-start(s8[9437184]{0:T(1024)(128)(4,1)} %bitcast.48), calls=%async_computation.5 | async-start | bytes 8388608
  695.6 16.4 %slice-start.2 = ((s8[9437184]{0:T(1024)(128)(4,1)}), s8[1048576]{0:T(1024)(128)(4,1)S(1)}, s32[]{:S(2)}) async-start(s8[9437184]{0:T(1024)(128)(4,1)} %bitcast.48), calls=%async_computation.6 | async-start | bytes 2097152
  733.7 10.9 %copy-start.5 = (f32[320,4]{1,0:T(8,128)S(1)}, f32[320,4]{1,0:T(8,128)}, u32[]{:S(2)}) copy-start(f32[320,4]{1,0:T(8,128)} %copy-done.4) | copy-start | bytes 15364
Sparse Core Ops, SparseCore 0:
  144.5 495.3 all-reduce.4
where the time goes:
time: 759 us; the launch traced here: 758 us
  waiting for transfers between devices  546 us (72%)
  matrix products  72.7 us (10%)
  other arithmetic  61.6 us (8%)
  local copies, waits for them, and re-layouts  49.4 us (7%)
  between operations  15 us (2%)
  starting transfers between devices  13.7 us (2%)
    psum x1, waiting for transfers between devices, body(): lax.psum(contract_last(token_slots, own_weights[0:2].reshape(2 * hidden_w...  495 us
    dot_general x3, matrix products, contract_first(): lax.dot_general(left_rows, right_rows, (((0,), (0,)), ((), ())), preferre...  36.9 us
    all_to_all x1, waiting for transfers between devices, body(): lax.all_to_all(send_grads, 'expert', split_axis=0, concat_axis=0, tiled=T...  33.2 us
    dot_general x2, matrix products, contract_last(): lax.dot_general(left_rows, right_rows, (((1,), (1,)), ((), ())), preferre...  25.5 us
    convert_element_type x1, other arithmetic, body(): update = step_dir.astype(jnp.bfloat16)[None]  21.6 us
    all_to_all x1, waiting for transfers between devices, body(): lax.all_to_all(send_tokens, 'expert', split_axis=0, concat_axis=0, tiled=...  17.6 us
  transfers between devices with their start and end apart: 7, of which 3 were waited for; matrix products, arithmetic and copies ran while one was open for 19% of the time, Pallas kernels for 0%

commit v1 on v0

--- a/solution.py
+++ b/solution.py
@@ -2,9 +2,15 @@
 import jax.numpy as jnp
 from jax import lax
 from jax.sharding import PartitionSpec as P
+from jax.lax import all_gather
 
 correction_one = 1.0 - 0.9**20
 correction_two = 1.0 - 0.95**20
+
+
+def try_all_rings_up(w_in):
+    state_now = all_gather(w_in, "tensor")
+    return jnp.sum(state_now, 0)
 
 
 def from_partner(value, axis, distance):
@@ -69,11 +75,10 @@
     grad_slots = got_grads.reshape(slot_rows, feat_width)
     own_weights = weights[0]
     hidden_width = own_weights.shape[1]
-    preact = lax.psum(
+    preact = try_all_rings_up(
         contract_last(token_slots, own_weights[0:2].reshape(2 * hidden_width, feat_width)).astype(
             jnp.bfloat16
-        ),
-        "tensor",
+        )
     ).astype(jnp.float32)
     gate_pre = preact[:, :hidden_width]
     up_pre = preact[:, hidden_width:]

time: 759 us -> 1010 us (1.33); the launches traced: 758 us -> 997 us
  waiting for transfers between devices: 546 us -> 718 us
  blocking collectives: 0 us -> 43.3 us
  other arithmetic: 61.6 us -> 82.7 us
    all_gather x0 -> x1, waiting for transfers between devices: none -> 578 us  [try_all_rings_up(): state_now = all_gather(w_in, 'tensor')]
    psum x1, waiting for transfers between devices: 495 us -> 114 us  [body(): lax.psum(contract_last(grad_slots, own_weights[2]).astype(jnp.bfloat16),...]
    all_to_all x0 -> x1, blocking collectives: none -> 43.3 us  [body(): lax.all_to_all(send_grads, 'expert', split_axis=0, concat_axis=0, tiled=T...]
    all_to_all x1 -> x0, waiting for transfers between devices: 33.2 us -> none  [body(): lax.all_to_all(send_grads, 'expert', split_axis=0, concat_axis=0, tiled=T...]
    reduce_sum x0 -> x1, other arithmetic: none -> 19.7 us  [try_all_rings_up(): return jnp.sum(state_now, 0)]
  transfers between devices with their start and end apart: 7 -> 7, of which waited for: 3 -> 3; matrix products, arithmetic and copies ran while one was open for 19% -> 17% of each run, Pallas kernels for 0% -> 0%
where the time goes in v1:
time: 1010 us; the launch traced here: 997 us
  waiting for transfers between devices  718 us (71%)
  other arithmetic  82.7 us (8%)
  matrix products  74.9 us (7%)
  local copies, waits for them, and re-layouts  53.4 us (5%)
  blocking collectives  43.3 us (4%)
  between operations  15.2 us (2%)
    all_gather x1, waiting for transfers between devices, try_all_rings_up(): state_now = all_gather(w_in, 'tensor')  578 us
    psum x1, waiting for transfers between devices, body(): lax.psum(contract_last(grad_slots, own_weights[2]).astype(jnp.bfloat16),...  114 us
    all_to_all x1, blocking collectives, body(): lax.all_to_all(send_grads, 'expert', split_axis=0, concat_axis=0, tiled=T...  43.3 us
    dot_general x3, matrix products, contract_first(): lax.dot_general(left_rows, right_rows, (((0,), (0,)), ((), ())), preferre...  39.2 us
    all_to_all x1, waiting for transfers between devices, body(): lax.all_to_all(send_tokens, 'expert', split_axis=0, concat_axis=0, tiled=...  25.4 us
    dot_general x2, matrix products, contract_last(): lax.dot_general(left_rows, right_rows, (((1,), (1,)), ((), ())), preferre...  25.4 us
    convert_element_type x1, other arithmetic, body(): update = step_dir.astype(jnp.bfloat16)[None]  21.6 us
  transfers between devices with their start and end apart: 7, of which 3 were waited for; matrix products, arithmetic and copies ran while one was open for 17% of the time, Pallas kernels for 0%

profile of v1, /device:TPU:0, one launch (start us, length us, event | category | flops | bytes accessed | tf_op | source)
XLA Modules:
  0.0 997.0 jit_solution(1538970550415856058)
XLA Ops:
  7.2 0.6 collective-permute-start
  7.7 0.8 copy.15
  8.6 0.1 eq.59
  8.7 0.7 broadcast_compare_fusion
  9.4 0.1 broadcast_in_dim.15
  9.4 0.1 eq.64
  9.5 0.1 select_reduce_fusion
  9.6 2.3 reduce-window.6
  11.9 0.3 slice_reduce_fusion
  12.2 0.2 reduce-window.9
  12.4 1.1 concatenate.25
  13.5 0.1 add_bitcast_fusion
  13.7 5.2 scatter_custom_fusion
  19.0 0.0 copy-start.8
  19.0 6.4 gather_fusion
  25.4 4.8 all-to-all-start
  30.3 0.0 all-gather.3.cloned.1.call-start
  30.3 0.6 fusion.30
  31.6 0.0 collective-permute-done
  31.6 5.4 broadcast_select_fusion
  37.1 0.0 copy-start
  37.1 3.7 copy-done
  40.8 3.4 slice.34
  44.2 25.4 %all-to-all-done = bf16[8,200,1024]{2,1,0:T(8,128)(2,1)S(1)} async-done(((bf16[8,200,1024]{2,1,0:T(8,128)(2,1)}), bf16[8,200,1024]{2,1,0:T(8,128)(2,1)S(1)}, u32[]{:S(2)}, u32[]{:S(2)}) %all-to-all-start) | async-done | bytes 3276832 | tf_op jit(solution)/shard_map/all_to_all | solution.py:70
  69.5 16.5 %convolution_convert_fusion = bf16[1600,3072]{1,0:T(8,128)(2,1)} fusion(bf16[1600,1024]{1,0:T(8,128)(2,1)S(1)} %bitcast.55, bf16[3072,1024]{1,0:T(8,128)(2,1)} %bitcast.54), kind=kOutput, calls=%fused_computation.14 | convolution fusion | flops 10071244800 | bytes 19398656 | tf_op jit(solution)/shard_map/dot_general | solution.py:21
  86.0 0.0 copy-done.2
  86.0 0.0 all-gather.3.cloned.1.call-update
  86.1 0.0 all-reduce.4.cloned.1.call-start
  86.1 0.6 copy-done.7
  86.7 0.1 copy.14
  86.9 0.0 copy-start.4
  86.9 0.1 mul.136
  87.0 0.1 copy-done.6
  87.1 3.8 mul.138
  90.9 7.9 mul.139
  98.8 4.3 multiply_convert_fusion.1
  103.1 0.2 concatenate.26
  103.4 6.4 gather_fusion.2
  109.8 43.3 %all_to_all.15 = bf16[8,200,1024]{2,1,0:T(8,128)(2,1)S(1)} all-to-all(bf16[8,200,1024]{2,1,0:T(8,128)(2,1)} %bitcast.49), channel_id=1, replica_groups=mesh['expert'=8,'tensor'=4] {'expert'}, dimensions={0} | all-to-all | bytes 6553600 | tf_op jit(solution)/shard_map/all_to_all | solution.py:71
  153.1 1.7 copy-done.3
  154.8 8.8 convolution_convert_fusion.1
  163.7 0.0 all-reduce.4.cloned.1.call-update
  163.7 0.1 collective-permute-start.1
  163.8 0.5 collective-permute-start.2
  164.3 578.5 %all-gather.3.cloned.1.call-done = bf16[6400,3072]{1,0:T(8,128)(2,1)} async-done(((bf16[1600,3072]{1,0:T(8,128)(2,1)}), bf16[6400,3072]{1,0:T(8,128)(2,1)}) %all-gather.3.cloned.1.call-update) | async-done | bytes 39321616 | tf_op jit(solution)/shard_map/all_gather | solution.py:12
  742.8 19.7 %reduce_sum.51 = bf16[1600,3072]{1,0:T(8,128)(2,1)} reduce(bf16[4,1600,3072]{2,1,0:T(8,128)(2,1)} %bitcast.47, bf16[]{:T(256)} %constant.22.clone.1), dimensions={0}, to_apply=%region_6.7 | reduce | flops 14745600 | bytes 49152000 | tf_op jit(solution)/shard_map/reduce_sum | solution.py:13
  762.5 12.8 %convert_element_type.66 = f32[1600,3072]{1,0:T(8,128)} convert(bf16[1600,3072]{1,0:T(8,128)(2,1)} %reduce_sum.51) | non-fusion elementwise | flops 4915200 | bytes 29491200 | tf_op jit(solution)/shard_map/convert_element_type | solution.py:82
  775.3 8.2 multiply_convert_fusion
  783.5 10.3 %convolution_convert_fusion.2 = bf16[1600,1024]{1,0:T(8,128)(2,1)} fusion(bf16[1600,1536]{1,0:T(8,128)(2,1)S(1)} %multiply_convert_fusion, bf16[1,3,1536,1024]{3,2,1,0:T(8,128)(2,1)} %copy-done), kind=kOutput, calls=%fused_computation.31 | convolution fusion | flops 5034803200 | bytes 11337728 | tf_op jit(solution)/shard_map/dot_general | solution.py:87
  793.8 3.8 all-to-all-start.1
  797.7 10.5 %convolution_bitcast_fusion = f32[1,1,1536,1024]{3,2,1,0:T(8,128)} fusion(bf16[1600,1536]{1,0:T(8,128)(2,1)} %copy-done.1, bf16[1600,1024]{1,0:T(8,128)(2,1)} %bitcast.59), kind=kOutput, calls=%fused_computation.30 | convolution fusion | flops 5033164800 | bytes 14483456 | tf_op jit(solution)/shard_map/dot_general | solution.py:27
  808.1 113.7 %all-reduce.4.cloned.1.call-done = bf16[1600,1536]{1,0:T(8,128)(2,1)} async-done(((bf16[1600,1536]{1,0:T(8,128)(2,1)}), bf16[1600,1536]{1,0:T(8,128)(2,1)}) %all-reduce.4.cloned.1.call-update) | async-done | bytes 4915216 | tf_op jit(solution)/shard_map/psum | solution.py:97
  921.9 12.2 %fusion.18 = f32[1,1,1536,1024]{3,2,1,0:T(8,128)} fusion(bf16[1600,1024]{1,0:T(8,128)(2,1)} %bitcast.56, bf16[1600,1536]{1,0:T(8,128)(2,1)} %all-reduce.4.cloned.1.call-done, f32[1600,3072]{1,0:T(8,128)} %convert_element_type.66), kind=kOutput, calls=%fused_computation.29 | convolution fusion | flops 5050368000 | bytes 24313856 | tf_op jit(solution)/shard_map/dot_general | solution.py:27
  934.1 16.5 %fusion.15 = f32[1,1,1536,1024]{3,2,1,0:T(8,128)} fusion(bf16[1600,1024]{1,0:T(8,128)(2,1)} %bitcast.57, bf16[1600,1536]{1,0:T(8,128)(2,1)} %all-reduce.4.cloned.1.call-done, f32[1600,3072]{1,0:T(8,128)} %convert_element_type.66), kind=kOutput, calls=%fused_computation.28 | convolution fusion | flops 5060198400 | bytes 34144256 | tf_op jit(solution)/shard_map/dot_general | solution.py:27
  950.6 0.0 collective-permute-done.1
  950.6 0.0 collective-permute-done.2
  950.6 0.0 slice-done
  950.6 0.0 slice-done.1
  950.6 0.0 slice-done.3
  950.6 21.6 %fusion.5 = bf16[1,3,1536,1024]{3,2,1,0:T(8,128)(2,1)} fusion(f32[1,1,1536,1024]{3,2,1,0:T(8,128)S(1)} %bitcast.53, f32[1,1,1536,1024]{3,2,1,0:T(8,128)} %fusion.18, f32[1,1,1536,1024]{3,2,1,0:T(8,128)} %fusion.15, bf16[1,3,1536,1024]{3,2,1,0:T(8,128)(2,1)} %collective-permute-done.2, bf16[1,3,1536,1024]{3,2,1,0:T(8,128)(2,1)S(1)} %bitcast.51, ...), kind=kLoop, calls=%fused_computation.11 | loop fusion | flops 84934656 | bytes 66060288 | tf_op jit(solution)/shard_map/convert_element_type | solution.py:114
  972.2 0.0 all-to-all-done.1
  972.2 5.1 gather_fusion.1
  977.3 5.9 reshape.227
  983.2 6.7 multiply_reduce_fusion
  (29 shorter events, 0.1 us)
Async XLA Ops:
  7.2 24.5 %collective-permute-start = (bf16[1,3,1536,1024]{3,2,1,0:T(8,128)(2,1)}, bf16[1,3,1536,1024]{3,2,1,0:T(8,128)(2,1)}, u32[]{:S(2)}, u32[]{:S(2)}) collective-permute-start(bf16[1,3,1536,1024]{3,2,1,0:T(8,128)(2,1)} %param.13), channel_id=1, source_target_pairs={{0,4},{4,0},{8,12},{12,8},{16,20},{20,16},{24,28},{28,24},{1,5},{5... | collective-permute-start | bytes 28311560 | tf_op jit(solution)/shard_map/ppermute | solution.py:17
  19.0 11.3 %copy-start.8 = (s32[4]{0:T(128)S(1)}, s32[4]{0:T(128)}, u32[]{:S(2)}) copy-start(s32[4]{0:T(128)} %param.12) | copy-start | bytes 52
  25.4 44.1 %all-to-all-start = ((bf16[8,200,1024]{2,1,0:T(8,128)(2,1)}), bf16[8,200,1024]{2,1,0:T(8,128)(2,1)S(1)}, u32[]{:S(2)}, u32[]{:S(2)}) async-start(bf16[8,200,1024]{2,1,0:T(8,128)(2,1)} %bitcast.48), calls=%async_computation | async-start | bytes 6553600 | tf_op jit(solution)/shard_map/all_to_all | solution.py:70
  30.3 712.5 %all-gather.3.cloned.1.call-start = ((), (), s32[]{:S(2)}) async-start(), calls=%async_computation.4 | async-start | bytes 49152000 | tf_op jit(solution)/shard_map/all_gather | solution.py:12
  37.1 3.7 copy-start
  69.5 16.5 %copy-start.2 = (bf16[8,200,1024]{2,1,0:T(8,128)(2,1)}, bf16[8,200,1024]{2,1,0:T(8,128)(2,1)S(1)}, u32[]{:S(2)}) copy-start(bf16[8,200,1024]{2,1,0:T(8,128)(2,1)S(1)} %all-to-all-done) | copy-start | bytes 9830404
  86.0 0.7 copy-start.7
  86.0 1.1 copy-start.6
  86.1 835.8 %all-reduce.4.cloned.1.call-start = ((), (), s32[]{:S(2)}) async-start(), calls=%async_computation.3 | async-start | bytes 9830400 | tf_op jit(solution)/shard_map/psum | solution.py:97
  86.9 11.9 %copy-start.4 = (f32[320,4]{1,0:T(8,128)}, f32[320,4]{1,0:T(8,128)S(1)}, u32[]{:S(2)}) copy-start(f32[320,4]{1,0:T(8,128)S(1)} %copy.14) | copy-start | bytes 15364
  153.1 1.7 copy-start.3
  163.7 786.9 %collective-permute-start.1 = (bf16[1,3,1536,1024]{3,2,1,0:T(8,128)(2,1)}, bf16[1,3,1536,1024]{3,2,1,0:T(8,128)(2,1)}, u32[]{:S(2)}, u32[]{:S(2)}) collective-permute-start(bf16[1,3,1536,1024]{3,2,1,0:T(8,128)(2,1)} %param.14), channel_id=1, source_target_pairs={{0,4},{4,0},{8,12},{12,8},{16,20},{20,16},{24,28},{28,24},{1,5},{5... | collective-permute-start | bytes 28311560 | tf_op jit(solution)/shard_map/ppermute | solution.py:17
  163.8 786.8 %collective-permute-start.2 = (bf16[1,3,1536,1024]{3,2,1,0:T(8,128)(2,1)}, bf16[1,3,1536,1024]{3,2,1,0:T(8,128)(2,1)}, u32[]{:S(2)}, u32[]{:S(2)}) collective-permute-start(bf16[1,3,1536,1024]{3,2,1,0:T(8,128)(2,1)} %param.15), channel_id=1, source_target_pairs={{0,4},{4,0},{8,12},{12,8},{16,20},{20,16},{24,28},{28,24},{1,5},{5... | collective-permute-start | bytes 28311560 | tf_op jit(solution)/shard_map/ppermute | solution.py:17
  783.5 10.3 %copy-start.1 = (bf16[1600,1536]{1,0:T(8,128)(2,1)}, bf16[1600,1536]{1,0:T(8,128)(2,1)S(1)}, u32[]{:S(2)}) copy-start(bf16[1600,1536]{1,0:T(8,128)(2,1)S(1)} %multiply_convert_fusion) | copy-start | bytes 14745604
  793.8 178.4 %all-to-all-start.1 = ((bf16[8,200,1024]{2,1,0:T(8,128)(2,1)}), bf16[8,200,1024]{2,1,0:T(8,128)(2,1)S(1)}, u32[]{:S(2)}, u32[]{:S(2)}) async-start(bf16[8,200,1024]{2,1,0:T(8,128)(2,1)} %bitcast.60), calls=%async_computation.1 | async-start | bytes 6553600 | tf_op jit(solution)/shard_map/all_to_all | solution.py:90
  921.9 28.7 %slice-start = ((s8[9437184]{0:T(1024)(128)(4,1)}), s8[4194304]{0:T(1024)(128)(4,1)S(1)}, s32[]{:S(2)}) async-start(s8[9437184]{0:T(1024)(128)(4,1)} %bitcast.50), calls=%async_computation.5 | async-start | bytes 8388608
  921.9 28.7 %slice-start.1 = ((s8[9437184]{0:T(1024)(128)(4,1)}), s8[4194304]{0:T(1024)(128)(4,1)S(1)}, s32[]{:S(2)}) async-start(s8[9437184]{0:T(1024)(128)(4,1)} %bitcast.50), calls=%async_computation.6 | async-start | bytes 8388608
  921.9 28.7 %slice-start.3 = ((s8[6291456]{0:T(1024)(128)(4,1)}), s8[4194304]{0:T(1024)(128)(4,1)S(1)}, s32[]{:S(2)}) async-start(s8[6291456]{0:T(1024)(128)(4,1)} %bitcast.52), calls=%async_computation.8 | async-start | bytes 8388608
  934.1 16.5 %slice-start.2 = ((s8[9437184]{0:T(1024)(128)(4,1)}), s8[1048576]{0:T(1024)(128)(4,1)S(1)}, s32[]{:S(2)}) async-start(s8[9437184]{0:T(1024)(128)(4,1)} %bitcast.50), calls=%async_computation.7 | async-start | bytes 2097152
  934.1 16.5 %slice-start.4 = ((s8[6291456]{0:T(1024)(128)(4,1)}), s8[2097152]{0:T(1024)(128)(4,1)S(1)}, s32[]{:S(2)}) async-start(s8[6291456]{0:T(1024)(128)(4,1)} %bitcast.52), calls=%async_computation.9 | async-start | bytes 4194304
  972.2 10.9 %copy-start.5 = (f32[320,4]{1,0:T(8,128)S(1)}, f32[320,4]{1,0:T(8,128)}, u32[]{:S(2)}) copy-start(f32[320,4]{1,0:T(8,128)} %copy-done.4) | copy-start | bytes 15364
Sparse Core Ops, SparseCore 0:
  86.2 656.5 all-gather.2
  745.1 176.6 all-reduce.3
